TPU v7x, 512 devices: a whole 4x8x8 slice. The times are simulated.
512 devices in a mesh: row: 32 (over z, y_lo), col: 16 (over y_hi, x, core).
Axes of the slice: x: 4, y: 8 (y_hi: 2, y_lo: 4; y = y_hi * 4 + y_lo), z: 8, core: 2. Of those that a mesh axis runs over, the one named last changes fastest.
Arguments:
- features: bfloat16 [16, 4096, 128], P('col', 'row'), may hold values from -6 to 6
- weight1: bfloat16 [128, 128], replicated, may hold values from -0.5 to 0.5
- weight2: bfloat16 [128, 128], replicated, may hold values from -0.5 to 0.5
- tile_values: bfloat16 [32, 16, 96, 128, 128], P('row', 'col'), may hold values from -0.1875 to 0.1875
- tile_coords: int32 [32, 16, 2, 96], P('row', 'col'), may hold values from 0 to 31, as said below
- tile_count: int32 [32, 16], P('row', 'col'), may hold values from 1 to 96, as said below
- out_grad: bfloat16 [16, 4096, 128], P('col', 'row'), may hold values from -6 to 6
Outputs:
- output: bfloat16 [16, 4096, 128], P('col', 'row')
- grad_features: bfloat16 [16, 4096, 128], P('col', 'row')
- grad_weight1: float32 [128, 128], replicated
- grad_weight2: float32 [128, 128], replicated
Inputs may be any that keep to these rules, and one draw needn't show every extreme that they name: On each device tile_coords[r, c, 0, t] is below 16 and tile_coords[r, c, 1, t] below 32; no block position appears twice among a device's 96 slots. `tile_count`: some device has all 96 slots live.
All inputs are finite; a program needn't handle non-finite values.
Results may differ from a plain program's by a relative error of at most 0.034.
Values may be sent and summed in bfloat16 or wider, within the bound.
No kernel may reach another device: no remote copies, remote signals or barrier semaphores. Data moves between devices by JAX's collectives and lax.ppermute only.
A program may use at most 64 MiB of HBM per device.

v0:
```python
import math
import jax
import jax.numpy as jnp
from jax import lax
from jax.sharding import PartitionSpec as P


def forward_part(local_tiles, row_ids, col_ids, live_slots, panel_rows, row_blocks):
    block_side = local_tiles.shape[1]
    feat_width = panel_rows.shape[-1]
    blocks = panel_rows.reshape(-1, block_side, feat_width)[col_ids]
    products = jnp.einsum("tij,tjf->tif", local_tiles, blocks, preferred_element_type=jnp.float32)
    onehot = jnp.where(
        (row_ids[None, :] == jnp.arange(row_blocks, dtype=jnp.int32)[:, None])
        & live_slots[None, :],
        1.0,
        0.0,
    ).astype(jnp.float32)
    return jnp.einsum("rt,tif->rif", onehot, products).reshape(row_blocks * block_side, feat_width)


def transposed_part(local_tiles, row_ids, col_ids, live_slots, panel_rows, col_blocks):
    block_side = local_tiles.shape[1]
    feat_width = panel_rows.shape[-1]
    blocks = panel_rows.reshape(-1, block_side, feat_width)[row_ids]
    products = jnp.einsum("tji,tjf->tif", local_tiles, blocks, preferred_element_type=jnp.float32)
    onehot = jnp.where(
        (col_ids[None, :] == jnp.arange(col_blocks, dtype=jnp.int32)[:, None])
        & live_slots[None, :],
        1.0,
        0.0,
    ).astype(jnp.float32)
    return jnp.einsum("ct,tif->cif", onehot, products).reshape(col_blocks * block_side, feat_width)


def silu_slope(value):
    sigmoid = jax.nn.sigmoid(value)
    return sigmoid * (1.0 + value * (1.0 - sigmoid))


def on_device(features, weight1, weight2, tile_values, tile_coords, tile_count, out_grad):
    local_tiles = tile_values[0, 0]
    row_ids = tile_coords[0, 0, 0]
    col_ids = tile_coords[0, 0, 1]
    slot_total = local_tiles.shape[0]
    live_slots = jnp.arange(slot_total, dtype=jnp.int32) < tile_count[0, 0]
    block_side = local_tiles.shape[1]
    shard_rows = features.shape[1]
    row_blocks = shard_rows * lax.axis_size("col") // block_side
    col_blocks = shard_rows * lax.axis_size("row") // block_side
    node_total = shard_rows * lax.axis_size("row") * lax.axis_size("col")
    grad_local = out_grad[0]
    grad_two = jnp.dot(grad_local, weight2.T, preferred_element_type=jnp.float32).astype(
        jnp.bfloat16
    )
    gathered = lax.all_gather(features, "row", axis=1, tiled=True)[0]
    grad_rows = lax.all_gather(grad_two, "row", axis=0, tiled=True)
    part_one = forward_part(local_tiles, row_ids, col_ids, live_slots, gathered, row_blocks)
    part_three = forward_part(local_tiles, row_ids, col_ids, live_slots, grad_rows, row_blocks)
    agg_sum, grad_hidden = (
        lax.psum_scatter(
            part_one.astype(jnp.bfloat16), "col", scatter_dimension=0, tiled=True
        ).astype(jnp.float32),
        lax.psum_scatter(
            part_three.astype(jnp.bfloat16), "col", scatter_dimension=0, tiled=True
        ).astype(jnp.float32),
    )
    agg_one = agg_sum.astype(jnp.bfloat16)
    pre_one = jnp.dot(agg_one, weight1, preferred_element_type=jnp.float32)
    hidden = jax.nn.silu(pre_one).astype(jnp.bfloat16)
    hidden_rows = lax.all_gather(hidden, "col", axis=0, tiled=True)
    part_two = transposed_part(local_tiles, row_ids, col_ids, live_slots, hidden_rows, col_blocks)
    agg_two = lax.psum_scatter(
        part_two.astype(jnp.bfloat16), "row", scatter_dimension=0, tiled=True
    )
    output = jnp.dot(agg_two, weight2, preferred_element_type=jnp.float32).astype(jnp.bfloat16)
    grad_pre = (grad_hidden * silu_slope(pre_one)).astype(jnp.bfloat16)
    grad_one = jnp.dot(grad_pre, weight1.T, preferred_element_type=jnp.float32).astype(jnp.bfloat16)
    grad_hidden_rows = lax.all_gather(grad_one, "col", axis=0, tiled=True)
    part_four = transposed_part(
        local_tiles, row_ids, col_ids, live_slots, grad_hidden_rows, col_blocks
    )
    grad_features = lax.psum_scatter(
        part_four.astype(jnp.bfloat16), "row", scatter_dimension=0, tiled=True
    )
    contract = (((0,), (0,)), ((), ()))
    weight_one = lax.dot_general(agg_one, grad_pre, contract, preferred_element_type=jnp.float32)
    weight_two = lax.dot_general(agg_two, grad_local, contract, preferred_element_type=jnp.float32)
    sum_one, sum_two = lax.psum((weight_one, weight_two), ("row", "col"))
    factor = 1.0 / math.sqrt(node_total)
    return (output[None], grad_features[None], sum_one * factor, sum_two * factor)


def solution(mesh):
    placed = (
        P("col", "row", None),
        P(),
        P(),
        P("row", "col", None, None, None),
        P("row", "col", None, None),
        P("row", "col"),
        P("col", "row", None),
    )
    return jax.shard_map(
        on_device,
        mesh=mesh,
        in_specs=placed,
        out_specs=(P("col", "row", None), P("col", "row", None), P(), P()),
        check_vma=False,
    )
```

profile of v0, /device:TPU:2, one launch (start us, length us, event | category | flops | bytes accessed | tf_op | source)
XLA Modules:
  0.0 1141.4 jit_solution(11435500891429155768)
XLA Ops:
  7.2 0.0 copy-start
  7.2 0.0 all-gather.5.cloned.1.call-start
  7.2 1.7 convolution_convert_fusion.1
  8.9 0.0 all-gather.5.cloned.1.call-update
  8.9 0.0 all-gather.3.cloned.1.call-start
  9.0 0.7 all-gather.3.cloned.1.call-update
  9.7 0.0 reduce-scatter.9.cloned.1.call-start
  10.4 0.8 fusion.63
  11.2 0.8 slice_bitcast_fusion.1
  11.9 156.6 %all-gather.5.cloned.1.call-done = bf16[4096,128]{1,0:T(8,128)(2,1)} async-done(((bf16[128,128]{1,0:T(8,128)(2,1)}), bf16[4096,128]{1,0:T(8,128)(2,1)}) %all-gather.5.cloned.1.call-update) | async-done | bytes 1048592 | tf_op jit(solution)/shard_map/all_gather | solution.py:57
  168.5 3.9 gather_fusion.2
  172.5 0.0 copy-done
  172.5 5.9 fusion.10
  178.4 5.0 copy.18
  183.3 2.4 fusion.25
  185.8 1.0 copy.14
  186.7 0.0 reduce-scatter.9.cloned.1.call-update
  186.7 0.0 reduce-scatter.5.cloned.1.call-start
  186.8 137.2 %all-gather.3.cloned.1.call-done = bf16[1,4096,128]{2,1,0:T(8,128)(2,1)} async-done(((bf16[1,128,128]{2,1,0:T(8,128)(2,1)}), bf16[1,4096,128]{2,1,0:T(8,128)(2,1)}) %all-gather.3.cloned.1.call-update) | async-done | bytes 1048592 | tf_op jit(solution)/shard_map/all_gather | solution.py:56
  324.0 3.9 gather_fusion
  327.9 5.9 fusion.14
  333.9 5.0 copy.16
  338.8 0.0 copy-start.4
  338.8 2.4 fusion.22
  341.2 1.0 copy.12
  342.2 0.0 reduce-scatter.5.cloned.1.call-update
  342.2 0.0 reduce-scatter.7.cloned.1.call-start
  342.3 71.1 %reduce-scatter.9.cloned.1.call-done = bf16[128,128]{1,0:T(8,128)(2,1)} async-done(((bf16[2048,128]{1,0:T(8,128)(2,1)}), bf16[128,128]{1,0:T(8,128)(2,1)}) %reduce-scatter.9.cloned.1.call-update) | async-done | bytes 32784 | tf_op jit(solution)/shard_map/reduce_scatter | solution.py:64
  413.4 86.4 %reduce-scatter.5.cloned.1.call-done = bf16[128,128]{1,0:T(8,128)(2,1)} async-done(((bf16[2048,128]{1,0:T(8,128)(2,1)}), bf16[128,128]{1,0:T(8,128)(2,1)}) %reduce-scatter.5.cloned.1.call-update) | async-done | bytes 32784 | tf_op jit(solution)/shard_map/reduce_scatter | solution.py:61
  499.8 0.0 copy-done.4
  499.8 0.9 multiply_convert_fusion
  500.8 27.9 %all_gather.13 = bf16[2048,128]{1,0:T(8,128)(2,1)} all-gather(bf16[128,128]{1,0:T(8,128)(2,1)S(1)} %get-tuple-element.7), channel_id=1, replica_groups=mesh['row'=32,'col'=16] {'col'}, dimensions={0}, use_global_device_ids=true | all-gather | bytes 557056 | tf_op jit(solution)/shard_map/all_gather | solution.py:71
  528.7 3.7 gather_fusion.1
  532.4 4.8 fusion.12
  537.2 5.0 copy.17
  542.2 2.4 fusion.16
  544.6 1.4 copy.13
  546.0 0.0 reduce-scatter.7.cloned.1.call-update
  546.0 0.0 all-reduce.3.cloned.1.call-start
  546.1 0.1 convolution_convert_fusion
  546.2 29.6 %all_gather.15 = bf16[2048,128]{1,0:T(8,128)(2,1)} all-gather(bf16[128,128]{1,0:T(8,128)(2,1)S(1)} %convolution_convert_fusion), channel_id=1, replica_groups=mesh['row'=32,'col'=16] {'col'}, dimensions={0}, use_global_device_ids=true | all-gather | bytes 557056 | tf_op jit(solution)/shard_map/all_gather | solution.py:79
  575.8 3.7 gather_fusion.3
  579.6 4.8 fusion.8
  584.4 0.0 copy-start.5
  584.4 0.0 copy-start.2
  584.4 5.0 copy.19
  589.3 0.0 copy-done.5
  589.3 0.8 fusion.72
  590.2 120.2 %reduce-scatter.7.cloned.1.call-done = bf16[128,128]{1,0:T(8,128)(2,1)} async-done(((bf16[4096,128]{1,0:T(8,128)(2,1)}), bf16[128,128]{1,0:T(8,128)(2,1)}) %reduce-scatter.7.cloned.1.call-update) | async-done | bytes 32784 | tf_op jit(solution)/shard_map/reduce_scatter | solution.py:73
  710.4 0.0 copy-done.2
  710.4 1.6 fusion.29
  712.0 0.0 all-reduce.3.cloned.1.call-update
  712.0 0.0 copy-start.1
  712.0 0.0 copy-start.3
  712.0 0.0 reduce-scatter.11.cloned.1.call-start
  712.0 2.4 fusion.19
  714.5 1.4 copy.15
  715.9 0.0 reduce-scatter.11.cloned.1.call-update
  715.9 0.0 copy-done.1
  715.9 0.0 copy-done.3
  715.9 0.8 fusion.28
  716.7 255.6 %all-reduce.3.cloned.1.call-done = (f32[128,128]{1,0:T(8,128)}, f32[128,128]{1,0:T(8,128)}) async-done(((f32[128,128]{1,0:T(8,128)}, f32[128,128]{1,0:T(8,128)}), (f32[128,128]{1,0:T(8,128)}, f32[128,128]{1,0:T(8,128)})) %all-reduce.3.cloned.1.call-update) | async-done | bytes 131088 | tf_op jit(solution)/shard_map/psum | solution.py:89
  972.2 1.5 broadcast_multiply_fusion
  973.8 160.8 %reduce-scatter.11.cloned.1.call-done = bf16[128,128]{1,0:T(8,128)(2,1)} async-done(((bf16[4096,128]{1,0:T(8,128)(2,1)}), bf16[128,128]{1,0:T(8,128)(2,1)}) %reduce-scatter.11.cloned.1.call-update) | async-done | bytes 32784 | tf_op jit(solution)/shard_map/reduce_scatter | solution.py:83
  (3 shorter events, 0.0 us)
Async XLA Ops:
  7.2 165.3 %copy-start = (bf16[1,1,96,128,128]{4,3,2,1,0:T(8,128)(2,1)S(1)}, bf16[1,1,96,128,128]{4,3,2,1,0:T(8,128)(2,1)}, u32[]{:S(2)}) copy-start(bf16[1,1,96,128,128]{4,3,2,1,0:T(8,128)(2,1)} %param.10) | copy-start | bytes 9437188
  7.2 161.4 %all-gather.5.cloned.1.call-start = ((), (), s32[]{:S(2)}) async-start(), calls=%async_computation.7 | async-start | bytes 1081344 | tf_op jit(solution)/shard_map/all_gather | solution.py:57
  8.9 315.1 %all-gather.3.cloned.1.call-start = ((), (), s32[]{:S(2)}) async-start(), calls=%async_computation.4 | async-start | bytes 1081344 | tf_op jit(solution)/shard_map/all_gather | solution.py:56
  9.7 403.7 %reduce-scatter.9.cloned.1.call-start = ((), (), s32[]{:S(2)}) async-start(), calls=%async_computation.8 | async-start | bytes 557056 | tf_op jit(solution)/shard_map/reduce_scatter | solution.py:64
  186.7 313.1 %reduce-scatter.5.cloned.1.call-start = ((), (), s32[]{:S(2)}) async-start(), calls=%async_computation.5 | async-start | bytes 557056 | tf_op jit(solution)/shard_map/reduce_scatter | solution.py:61
  338.8 161.0 %copy-start.4 = (bf16[128,128]{1,0:T(8,128)(2,1)S(1)}, bf16[128,128]{1,0:T(8,128)(2,1)}, u32[]{:S(2)}) copy-start(bf16[128,128]{1,0:T(8,128)(2,1)} %param.8) | copy-start | bytes 98308
  342.2 368.2 %reduce-scatter.7.cloned.1.call-start = ((), (), s32[]{:S(2)}) async-start(), calls=%async_computation.6 | async-start | bytes 1081344 | tf_op jit(solution)/shard_map/reduce_scatter | solution.py:73
  546.0 426.2 %all-reduce.3.cloned.1.call-start = ((), (), s32[]{:S(2)}) async-start(), calls=%async_computation.10 | async-start | bytes 262144 | tf_op jit(solution)/shard_map/psum | solution.py:89
  584.4 5.0 copy-start.5
  584.4 126.0 %copy-start.2 = (bf16[1,128,128]{2,1,0:T(8,128)(2,1)S(1)}, bf16[1,128,128]{2,1,0:T(8,128)(2,1)}, u32[]{:S(2)}) copy-start(bf16[1,128,128]{2,1,0:T(8,128)(2,1)} %param.13) | copy-start | bytes 98308
  712.0 3.9 copy-start.1
  712.0 3.9 copy-start.3
  712.0 422.6 %reduce-scatter.11.cloned.1.call-start = ((), (), s32[]{:S(2)}) async-start(), calls=%async_computation.9 | async-start | bytes 1081344 | tf_op jit(solution)/shard_map/reduce_scatter | solution.py:83
Sparse Core Ops, SparseCore 0:
  10.7 157.8 all-gather.4
  170.6 153.3 all-gather.2
  328.7 84.6 reduce-scatter.8
  418.5 81.2 reduce-scatter.4
  546.1 164.1 reduce-scatter.6
  716.9 255.3 all-reduce.2
  975.6 158.9 reduce-scatter.10
where the time goes:
time: 1140 us
  waiting for transfers between devices  989 us (87%)
  blocking collectives  57.6 us (5%)
  local copies, waits for them, and re-layouts  40.6 us (4%)
  matrix products  37 us (3%)
  between operations  14.9 us (1%)
    psum x1, waiting for transfers between devices, on_device(): sum_one, sum_two = lax.psum((weight_one, weight_two), ('row', 'col'))  256 us
    reduce_scatter x1, waiting for transfers between devices, on_device(): lax.psum_scatter(part_four.astype(jnp.bfloat16), 'row', scatter_dimension...  161 us
    all_gather x1, waiting for transfers between devices, on_device(): grad_rows = lax.all_gather(grad_two, 'row', axis=0, tiled=True)  157 us
    all_gather x1, waiting for transfers between devices, on_device(): gathered = lax.all_gather(features, 'row', axis=1, tiled=True)[0]  137 us
    reduce_scatter x1, waiting for transfers between devices, on_device(): lax.psum_scatter(part_two.astype(jnp.bfloat16), 'row', scatter_dimension=...  120 us
    reduce_scatter x1, waiting for transfers between devices, on_device(): lax.psum_scatter(part_one.astype(jnp.bfloat16), 'col', scatter_dimension=...  86.4 us
    reduce_scatter x1, waiting for transfers between devices, on_device(): lax.psum_scatter(part_three.astype(jnp.bfloat16), 'col', scatter_dimensio...  71.1 us
    all_gather x1, blocking collectives, on_device(): grad_hidden_rows = lax.all_gather(grad_one, 'col', axis=0, tiled=True)  29.6 us
  transfers between devices with their start and end apart: 7, of which 7 were waited for; matrix products, arithmetic and copies ran while one was open for 5% of the time, Pallas kernels for 0%

commit v1 on v0

--- a/solution.py
+++ b/solution.py
@@ -3,6 +3,11 @@
 import jax.numpy as jnp
 from jax import lax
 from jax.sharding import PartitionSpec as P
+
+
+def one_after_other(value_2, one, other):
+    partial = lax.psum(value_2, one)
+    return lax.psum(partial, other)
 
 
 def forward_part(local_tiles, row_ids, col_ids, live_slots, panel_rows, row_blocks):
@@ -86,7 +91,7 @@
     contract = (((0,), (0,)), ((), ()))
     weight_one = lax.dot_general(agg_one, grad_pre, contract, preferred_element_type=jnp.float32)
     weight_two = lax.dot_general(agg_two, grad_local, contract, preferred_element_type=jnp.float32)
-    sum_one, sum_two = lax.psum((weight_one, weight_two), ("row", "col"))
+    sum_one, sum_two = one_after_other((weight_one, weight_two), "row", "col")
     factor = 1.0 / math.sqrt(node_total)
     return (output[None], grad_features[None], sum_one * factor, sum_two * factor)
 

time: 1140 us -> 1350 us (1.18)
  the two profiles are of different devices: /device:TPU:2 before, /device:TPU:6 now
where the time goes in v1:
time: 1350 us
  waiting for transfers between devices  1200 us (89%)
  blocking collectives  55.9 us (4%)
  local copies, waits for them, and re-layouts  40.5 us (3%)
  matrix products  37 us (3%)
  between operations  14.9 us (1%)
    psum x1, waiting for transfers between devices, one_after_other(): partial = lax.psum(value_2, one)  270 us
    psum x1, waiting for transfers between devices, one_after_other(): return lax.psum(partial, other)  174 us
    reduce_scatter x1, waiting for transfers between devices, on_device(): lax.psum_scatter(part_four.astype(jnp.bfloat16), 'row', scatter_dimension...  169 us
    all_gather x1, waiting for transfers between devices, on_device(): grad_rows = lax.all_gather(grad_two, 'row', axis=0, tiled=True)  157 us
    all_gather x1, waiting for transfers between devices, on_device(): gathered = lax.all_gather(features, 'row', axis=1, tiled=True)[0]  137 us
    reduce_scatter x1, waiting for transfers between devices, on_device(): lax.psum_scatter(part_two.astype(jnp.bfloat16), 'row', scatter_dimension=...  132 us
    reduce_scatter x1, waiting for transfers between devices, on_device(): lax.psum_scatter(part_one.astype(jnp.bfloat16), 'col', scatter_dimension=...  86.5 us
    reduce_scatter x1, waiting for transfers between devices, on_device(): lax.psum_scatter(part_three.astype(jnp.bfloat16), 'col', scatter_dimensio...  70.8 us
  transfers between devices with their start and end apart: 8, of which 8 were waited for; matrix products, arithmetic and copies ran while one was open for 4% of the time, Pallas kernels for 0%

profile of v1, /device:TPU:6, one launch (start us, length us, event | category | flops | bytes accessed | tf_op | source)
XLA Modules:
  0.0 1347.9 jit_solution(10883201379877712381)
XLA Ops:
  7.2 0.0 copy-start
  7.2 0.0 all-gather.5.cloned.1.call-start
  7.2 1.7 convolution_convert_fusion.1
  8.9 0.0 all-gather.5.cloned.1.call-update
  8.9 0.0 all-gather.3.cloned.1.call-start
  9.0 0.7 all-gather.3.cloned.1.call-update
  9.7 0.0 reduce-scatter.9.cloned.1.call-start
  10.4 0.8 fusion.63
  11.2 0.8 slice_bitcast_fusion.1
  11.9 156.7 %all-gather.5.cloned.1.call-done = bf16[4096,128]{1,0:T(8,128)(2,1)} async-done(((bf16[128,128]{1,0:T(8,128)(2,1)}), bf16[4096,128]{1,0:T(8,128)(2,1)}) %all-gather.5.cloned.1.call-update) | async-done | bytes 1048592 | tf_op jit(solution)/shard_map/all_gather | solution.py:62
  168.6 3.9 gather_fusion.2
  172.5 0.0 copy-done
  172.5 5.9 fusion.10
  178.5 4.9 copy.18
  183.4 2.4 fusion.25
  185.8 1.0 copy.14
  186.8 0.0 reduce-scatter.9.cloned.1.call-update
  186.8 0.0 reduce-scatter.5.cloned.1.call-start
  186.8 137.4 %all-gather.3.cloned.1.call-done = bf16[1,4096,128]{2,1,0:T(8,128)(2,1)} async-done(((bf16[1,128,128]{2,1,0:T(8,128)(2,1)}), bf16[1,4096,128]{2,1,0:T(8,128)(2,1)}) %all-gather.3.cloned.1.call-update) | async-done | bytes 1048592 | tf_op jit(solution)/shard_map/all_gather | solution.py:61
  324.2 3.9 gather_fusion
  328.2 5.9 fusion.14
  334.1 4.9 copy.16
  339.0 2.4 fusion.22
  341.4 0.9 copy.12
  342.4 0.0 reduce-scatter.5.cloned.1.call-update
  342.4 0.0 reduce-scatter.7.cloned.1.call-start
  342.4 70.8 %reduce-scatter.9.cloned.1.call-done = bf16[128,128]{1,0:T(8,128)(2,1)} async-done(((bf16[2048,128]{1,0:T(8,128)(2,1)}), bf16[128,128]{1,0:T(8,128)(2,1)}) %reduce-scatter.9.cloned.1.call-update) | async-done | bytes 32784 | tf_op jit(solution)/shard_map/reduce_scatter | solution.py:69
  413.3 86.5 %reduce-scatter.5.cloned.1.call-done = bf16[128,128]{1,0:T(8,128)(2,1)} async-done(((bf16[2048,128]{1,0:T(8,128)(2,1)}), bf16[128,128]{1,0:T(8,128)(2,1)}) %reduce-scatter.5.cloned.1.call-update) | async-done | bytes 32784 | tf_op jit(solution)/shard_map/reduce_scatter | solution.py:66
  499.7 0.0 copy-done.4
  499.7 0.9 multiply_convert_fusion
  500.7 26.3 %all_gather.13 = bf16[2048,128]{1,0:T(8,128)(2,1)} all-gather(bf16[128,128]{1,0:T(8,128)(2,1)S(1)} %get-tuple-element.9), channel_id=1, replica_groups=mesh['row'=32,'col'=16] {'col'}, dimensions={0}, use_global_device_ids=true | all-gather | bytes 557056 | tf_op jit(solution)/shard_map/all_gather | solution.py:76
  527.0 3.7 gather_fusion.1
  530.8 4.8 fusion.12
  535.5 4.9 copy.17
  540.5 2.4 fusion.16
  542.9 1.4 copy.13
  544.3 0.0 reduce-scatter.7.cloned.1.call-update
  544.3 0.0 all-reduce.5.cloned.1.call-start
  544.4 0.1 convolution_convert_fusion
  544.5 29.6 %all_gather.15 = bf16[2048,128]{1,0:T(8,128)(2,1)} all-gather(bf16[128,128]{1,0:T(8,128)(2,1)S(1)} %convolution_convert_fusion), channel_id=1, replica_groups=mesh['row'=32,'col'=16] {'col'}, dimensions={0}, use_global_device_ids=true | all-gather | bytes 557056 | tf_op jit(solution)/shard_map/all_gather | solution.py:84
  574.1 3.8 gather_fusion.3
  577.8 0.0 copy-done.5
  577.8 0.8 fusion.72
  578.6 131.6 %reduce-scatter.7.cloned.1.call-done = bf16[128,128]{1,0:T(8,128)(2,1)} async-done(((bf16[4096,128]{1,0:T(8,128)(2,1)}), bf16[128,128]{1,0:T(8,128)(2,1)}) %reduce-scatter.7.cloned.1.call-update) | async-done | bytes 32784 | tf_op jit(solution)/shard_map/reduce_scatter | solution.py:78
  710.3 0.0 copy-done.2
  710.3 1.6 fusion.29
  711.9 0.0 all-reduce.5.cloned.1.call-update
  711.9 0.2 all-reduce.7.cloned.1.call-start
  712.1 4.8 fusion.8
  716.9 4.9 copy.19
  721.8 270.4 %all-reduce.5.cloned.1.call-done = (f32[128,128]{1,0:T(8,128)}, f32[128,128]{1,0:T(8,128)}) async-done(((f32[128,128]{1,0:T(8,128)}, f32[128,128]{1,0:T(8,128)}), (f32[128,128]{1,0:T(8,128)}, f32[128,128]{1,0:T(8,128)})) %all-reduce.5.cloned.1.call-update) | async-done | bytes 131088 | tf_op jit(solution)/shard_map/psum | solution.py:9
  992.3 0.0 all-reduce.7.cloned.1.call-update
  992.3 0.0 copy-start.1
  992.3 0.0 copy-start.3
  992.3 0.0 reduce-scatter.11.cloned.1.call-start
  992.4 2.4 fusion.19
  994.8 1.4 copy.15
  996.2 0.0 reduce-scatter.11.cloned.1.call-update
  996.2 0.0 copy-done.1
  996.2 0.0 copy-done.3
  996.2 0.8 fusion.28
  997.0 173.5 %all-reduce.7.cloned.1.call-done = (f32[128,128]{1,0:T(8,128)}, f32[128,128]{1,0:T(8,128)}) async-done(((f32[128,128]{1,0:T(8,128)}, f32[128,128]{1,0:T(8,128)}), (f32[128,128]{1,0:T(8,128)}, f32[128,128]{1,0:T(8,128)})) %all-reduce.7.cloned.1.call-update) | async-done | bytes 131088 | tf_op jit(solution)/shard_map/psum | solution.py:10
  1170.5 1.5 broadcast_multiply_fusion
  1172.1 169.0 %reduce-scatter.11.cloned.1.call-done = bf16[128,128]{1,0:T(8,128)(2,1)} async-done(((bf16[4096,128]{1,0:T(8,128)(2,1)}), bf16[128,128]{1,0:T(8,128)(2,1)}) %reduce-scatter.11.cloned.1.call-update) | async-done | bytes 32784 | tf_op jit(solution)/shard_map/reduce_scatter | solution.py:88
  (6 shorter events, 0.0 us)
Async XLA Ops:
  7.2 165.4 %copy-start = (bf16[1,1,96,128,128]{4,3,2,1,0:T(8,128)(2,1)S(1)}, bf16[1,1,96,128,128]{4,3,2,1,0:T(8,128)(2,1)}, u32[]{:S(2)}) copy-start(bf16[1,1,96,128,128]{4,3,2,1,0:T(8,128)(2,1)} %param.10) | copy-start | bytes 9437188
  7.2 161.4 %all-gather.5.cloned.1.call-start = ((), (), s32[]{:S(2)}) async-start(), calls=%async_computation.7 | async-start | bytes 1081344 | tf_op jit(solution)/shard_map/all_gather | solution.py:62
  8.9 315.3 %all-gather.3.cloned.1.call-start = ((), (), s32[]{:S(2)}) async-start(), calls=%async_computation.4 | async-start | bytes 1081344 | tf_op jit(solution)/shard_map/all_gather | solution.py:61
  9.7 403.6 %reduce-scatter.9.cloned.1.call-start = ((), (), s32[]{:S(2)}) async-start(), calls=%async_computation.8 | async-start | bytes 557056 | tf_op jit(solution)/shard_map/reduce_scatter | solution.py:69
  186.8 312.9 %reduce-scatter.5.cloned.1.call-start = ((), (), s32[]{:S(2)}) async-start(), calls=%async_computation.5 | async-start | bytes 557056 | tf_op jit(solution)/shard_map/reduce_scatter | solution.py:66
  339.0 160.7 %copy-start.4 = (bf16[128,128]{1,0:T(8,128)(2,1)S(1)}, bf16[128,128]{1,0:T(8,128)(2,1)}, u32[]{:S(2)}) copy-start(bf16[128,128]{1,0:T(8,128)(2,1)} %param.8) | copy-start | bytes 98308
  342.4 367.9 %reduce-scatter.7.cloned.1.call-start = ((), (), s32[]{:S(2)}) async-start(), calls=%async_computation.6 | async-start | bytes 1081344 | tf_op jit(solution)/shard_map/reduce_scatter | solution.py:78
  544.3 447.9 %all-reduce.5.cloned.1.call-start = ((), (), s32[]{:S(2)}) async-start(), calls=%async_computation.10 | async-start | bytes 262144 | tf_op jit(solution)/shard_map/psum | solution.py:9
  574.1 3.8 copy-start.5
  574.1 136.2 %copy-start.2 = (bf16[1,128,128]{2,1,0:T(8,128)(2,1)S(1)}, bf16[1,128,128]{2,1,0:T(8,128)(2,1)}, u32[]{:S(2)}) copy-start(bf16[1,128,128]{2,1,0:T(8,128)(2,1)} %param.13) | copy-start | bytes 98308
  711.9 458.6 %all-reduce.7.cloned.1.call-start = ((), (), s32[]{:S(2)}) async-start(), calls=%async_computation.11 | async-start | bytes 262144 | tf_op jit(solution)/shard_map/psum | solution.py:10
  992.3 3.9 copy-start.1
  992.3 3.9 copy-start.3
  992.3 348.7 %reduce-scatter.11.cloned.1.call-start = ((), (), s32[]{:S(2)}) async-start(), calls=%async_computation.9 | async-start | bytes 1081344 | tf_op jit(solution)/shard_map/reduce_scatter | solution.py:88
Sparse Core Ops, SparseCore 0:
  10.7 157.8 all-gather.4
  170.7 153.4 all-gather.2
  328.9 84.3 reduce-scatter.8
  418.4 81.2 reduce-scatter.4
  544.5 165.7 reduce-scatter.6
  714.0 278.2 all-reduce.4
  995.2 175.2 all-reduce.6
  1174.1 166.8 reduce-scatter.10
